TPU v7x, 32 devices: a whole 2x2x4 slice. The times are simulated.
32 devices in a mesh: grid: 8 (over y, x, core), pt: 4 (over z).
Axes of the slice: x: 2, y: 2, z: 4, core: 2. Of those that a mesh axis runs over, the one named last changes fastest.
Arguments:
- orbitals: bfloat16 [2048, 4096], P('grid'), may hold values from -0.875 to 0.875
- point_index: int32 [2048], P('pt'), may hold values from 0 to 4095, as said below
- factor_panels: float32 [2048, 1024], P('pt'), as said below
Outputs:
- solved: float32 [4096, 2048], P('grid', 'pt')
Inputs may be any that keep to these rules, and one draw needn't show every extreme that they name: `point_index`: all entries are different; 0 and 4095 are always among them. `factor_panels`: lower triangular in its global row and column indices, diagonal between 1.5 and 3.
All inputs are finite; a program needn't handle non-finite values.
Results may differ from a plain program's by a relative error of at most 0.0018.
Values may be sent and summed in bfloat16 or wider, within the bound.
A program may use at most 64 MiB of HBM per device.

v0:
```python
import functools
import jax
import jax.numpy as jnp
from jax import lax
from jax.experimental import pallas as pl
from jax.experimental.pallas import tpu as pltpu
from jax.sharding import PartitionSpec as P

MESH = pl.DeviceIdType.MESH
F32, BF16 = jnp.float32, jnp.bfloat16
LANES = 128
PIECE = 32


def split(value):
    high = value.astype(BF16)
    return high, (value - high.astype(F32)).astype(BF16)


def dot(a, b):
    return jnp.dot(a, b, preferred_element_type=F32)


def exact_dot(a, b):
    return jnp.dot(a, b, preferred_element_type=F32, precision=lax.Precision.HIGHEST)


def invert_lower(low, inv):
    size = low.shape[0]
    blocks = size // LANES
    row = lax.broadcasted_iota(jnp.int32, (LANES, LANES), 0)
    col = lax.broadcasted_iota(jnp.int32, (LANES, LANES), 1)
    tiles, parts = [], []
    for i in range(blocks):
        at = slice(i * LANES, (i + 1) * LANES)
        tile = low[at, at]
        tiles.append(tile)
        parts.append(jnp.where(row == col, 1.0 / jnp.where(row == col, tile, 1.0), 0.0))
    half = 1
    level = 0
    while half < LANES:
        rb, cb = row >> level, col >> level
        mask = ((rb >> 1) == (cb >> 1)) & (rb > cb)
        mids = [exact_dot(jnp.where(mask, tiles[i], 0.0), parts[i]) for i in range(blocks)]
        parts = [parts[i] - exact_dot(parts[i], mids[i]) for i in range(blocks)]
        half *= 2
        level += 1
    inv[...] = jnp.zeros_like(inv)
    for i in range(blocks):
        at = slice(i * LANES, (i + 1) * LANES)
        inv[at, at] = parts[i]
    width = LANES
    while width < size:
        for start in range(0, size, 2 * width):
            top = slice(start, start + width)
            bottom = slice(start + width, start + 2 * width)
            mid = exact_dot(low[bottom, top], inv[top, top])
            inv[bottom, top] = -exact_dot(inv[bottom, bottom], mid)
        width *= 2


def kernel(
    grid_count, pt_count, index_ref, orb, fac, out,
    orb_v, fac_v, rows, points, gathered, low, inv, a_high, a_low, b_high, b_low, firsts, seconds,
    load_sem, own_sem, row_send, row_recv, sibling_recv, late_send, help_send, help_recv,
    point_send, point_recv, pass_send,
    first_send, first_recv, second_send, second_recv,
):
    me = lax.axis_index("grid")
    rank = lax.axis_index("pt")
    own_bands, grid_rows = orb.shape
    half_bands = own_bands // 2
    chunks = rows.shape[0]
    panel = index_ref.shape[1]
    rows_here = chunks * LANES
    partner = me + 1 - 2 * lax.rem(me, 2)
    chip = me - lax.rem(me, 2)
    pairs = grid_count // 2
    far = grid_count - 2
    last = pt_count - 1
    mine = lax.rem(pt_count - rank, 2)

    def block(g):
        return pl.ds(pl.multiple_of(g * half_bands, half_bands), half_bands)

    def half_of(h):
        return pl.ds(pl.multiple_of(h * half_bands, half_bands), half_bands)

    def far_one(i):
        return lax.rem(chip + 2 + i, grid_count)

    load_orb = pltpu.make_async_copy(orb, orb_v, load_sem.at[0])
    load_fac = pltpu.make_async_copy(fac, fac_v, load_sem.at[1])
    load_orb.start()

    barrier = pltpu.get_barrier_semaphore()

    @pl.loop(1, grid_count)
    def _(k):
        other = lax.rem(me + k, grid_count)
        pl.semaphore_signal(barrier, inc=1, device_id=(other, rank), device_id_type=MESH)

    @pl.when(rank > 0)
    def _():
        pl.semaphore_signal(barrier, inc=1, device_id=(me, rank - 1), device_id_type=MESH)

    @pl.when(rank < last)
    def _():
        pl.semaphore_signal(barrier, inc=1, device_id=(me, rank + 1), device_id_type=MESH)

    at_end = (rank == 0) | (rank == last)

    @pl.when(at_end)
    def _():
        pl.semaphore_wait(barrier, grid_count)

    @pl.when(jnp.logical_not(at_end))
    def _():
        pl.semaphore_wait(barrier, grid_count + 1)

    def row_cols(g, c):
        return pl.ds(pl.multiple_of(g * rows_here + c * LANES, LANES), LANES)

    def row_copy(c, h, target, send_sem, recv_sem):
        return pltpu.make_async_remote_copy(
            src_ref=orb.at[half_of(h), row_cols(target, c)],
            dst_ref=rows.at[c, h, block(me), :],
            send_sem=send_sem.at[c],
            recv_sem=recv_sem.at[c],
            device_id=(target, rank),
            device_id_type=MESH,
        )

    def send_rows(c):
        @pl.loop(0, far)
        def _(i):
            row_copy(c, mine, far_one(i), row_send, row_recv).start()

        row_copy(c, 0, partner, row_send, sibling_recv).start()
        row_copy(c, 1, partner, row_send, sibling_recv).start()

    send_rows(0)
    for c in range(chunks):
        for h in range(2):
            pltpu.make_async_copy(
                orb.at[half_of(h), row_cols(me, c)], rows.at[c, h, block(me), :], own_sem.at[c]
            ).start()
    load_fac.start()
    load_orb.wait()

    depth = min(1024, grid_rows)
    gathered[...] = jnp.zeros_like(gathered)

    @pl.loop(0, grid_rows // depth)
    def _(s):
        ids = lax.broadcasted_iota(jnp.int32, (depth, panel), 0) + s * depth
        hot = jnp.where(ids == index_ref[...], 1.0, 0.0).astype(BF16)
        gathered[...] += dot(orb_v[:, pl.ds(pl.multiple_of(s * depth, depth), depth)], hot)

    points[0, block(me), :] = gathered[0:half_bands, :].astype(BF16)
    points[1, block(me), :] = gathered[half_bands:own_bands, :].astype(BF16)

    def point_copy(g, target, send_sem):
        return pltpu.make_async_remote_copy(
            src_ref=points.at[:, block(g), :],
            dst_ref=points.at[:, block(g), :],
            send_sem=send_sem,
            recv_sem=point_recv.at[g],
            device_id=(target, rank),
            device_id_type=MESH,
        )

    @pl.loop(1, pairs)
    def _(k):
        point_copy(me, lax.rem(me + 2 * k, grid_count), point_send.at[k]).start()

    point_copy(me, partner, pass_send.at[0]).start()
    if chunks > 1:
        send_rows(1)

    def settle(c, count, sem):
        part = rows.at[c, 0, pl.ds(0, count), :]
        pltpu.make_async_copy(part, part, sem.at[c]).wait()

    def send_late(c):
        @pl.when(rank == last)
        def _():
            @pl.loop(0, far)
            def _(i):
                row_copy(c, 1 - mine, far_one(i), late_send, help_recv).start()

    def push(c):
        settle(c - 2, grid_count * half_bands, row_send)
        send_rows(c)
        send_late(c - 2)

    def forward(c):
        settle(c, far * half_bands, row_recv)

        @pl.when(rank > 0)
        def _():
            @pl.loop(0, far)
            def _(i):
                part = rows.at[c, mine, block(far_one(i)), :]
                pltpu.make_async_remote_copy(
                    src_ref=part,
                    dst_ref=part,
                    send_sem=help_send.at[c],
                    recv_sem=help_recv.at[c],
                    device_id=(me, rank - 1),
                    device_id_type=MESH,
                ).start()

    @pl.when(rank > 0)
    def _():
        forward(0)

    load_fac.wait()

    @pl.when(rank < 2)
    def _():
        start = pl.multiple_of(rank * panel, panel)
        low[...] = fac_v[:, pl.ds(start, panel)]
        invert_lower(low, inv)

    @pl.when(rank > 0)
    def _():
        a_high[...], a_low[...] = split(fac_v[:, 0:panel].T)

    @pl.when(rank == 0)
    def _():
        a_high[...], a_low[...] = split(inv[...].T)

    @pl.when(rank > 1)
    def _():
        b_high[...], b_low[...] = split(fac_v[:, panel : 2 * panel].T)

    @pl.when(rank == 1)
    def _():
        b_high[...], b_low[...] = split(inv[...].T)

    @pl.loop(1, pairs)
    def _(k):
        source = lax.rem(me + 2 * (pairs - k), grid_count)
        point_copy(source, me, point_send.at[k]).wait_recv()
        point_copy(source, partner, pass_send.at[k]).start()

    @pl.loop(1, pairs)
    def _(k):
        point_copy(me, partner, point_send.at[k]).wait_send()

    if chunks > 2:
        push(2)
    for c in range(1, chunks):

        @pl.when(rank > c)
        def _():
            forward(c)

        if c + 2 < chunks:

            @pl.when(rank > 1)
            def _():
                push(c + 2)

    for c in range(max(chunks - 2, 0), chunks):
        send_late(c)

    @pl.loop(0, pairs)
    def _(k):
        source = lax.rem(partner + 2 * k, grid_count)
        point_copy(source, me, pass_send.at[k]).wait_recv()

    def chain(buf, p, send_sem, recv_sem):
        return pltpu.make_async_remote_copy(
            src_ref=buf.at[p],
            dst_ref=buf.at[p],
            send_sem=send_sem.at[p],
            recv_sem=recv_sem.at[p],
            device_id=(me, rank + 1),
            device_id_type=MESH,
        )

    def solve(value, high, low_part):
        value_high, value_low = split(value)
        return dot(value_high, high[...]) + (dot(value_high, low_part[...]) + dot(value_low, high[...]))

    def apply(value, high, low_part):
        return dot(value, high[...]) + dot(value, low_part[...])

    piece = firsts.shape[1]
    pieces = LANES // piece

    @pl.loop(0, chunks)
    def _(c):
        @pl.when(c + rank < chunks)
        def _():
            forward(c + rank)

        settle(c, own_bands, own_sem)
        settle(c, own_bands, sibling_recv)
        settle(c, far * half_bands, help_recv)
        over_bands = (((0,), (0,)), ((), ()))
        sums = lax.dot_general(rows[c, 0], points[0], over_bands, preferred_element_type=F32)
        sums += lax.dot_general(rows[c, 1], points[1], over_bands, preferred_element_type=F32)
        out[pl.ds(pl.multiple_of(c * LANES, LANES), LANES), :] = sums * sums

        @pl.when((rank < 2) & (c + 3 < chunks))
        def _():
            push(c + 3)

        @pl.loop(c * pieces, (c + 1) * pieces)
        def _(p):
            here = pl.ds(pl.multiple_of(p * piece, piece), piece)

            @pl.when(rank == 0)
            def _():
                first = solve(out[here, :], a_high, a_low)
                out[here, :] = first
                firsts[p] = first.astype(BF16)

            @pl.when(rank > 0)
            def _():
                chain(firsts, p, first_send, first_recv).wait_recv()

            @pl.when(rank < last)
            def _():
                chain(firsts, p, first_send, first_recv).start()

            @pl.when(rank > 0)
            def _():
                out[here, :] -= apply(firsts[p], a_high, a_low)

            @pl.when(rank == 1)
            def _():
                second = solve(out[here, :], b_high, b_low)
                out[here, :] = second
                seconds[p] = second.astype(BF16)

            @pl.when(rank > 1)
            def _():
                chain(seconds, p, second_send, second_recv).wait_recv()

            @pl.when((rank > 0) & (rank < last))
            def _():
                chain(seconds, p, second_send, second_recv).start()

            @pl.when(rank > 1)
            def _():
                out[here, :] -= apply(seconds[p], b_high, b_low)

    @pl.loop(0, chunks)
    def _(c):
        @pl.when(c >= chunks - 2)
        def _():
            settle(c, grid_count * half_bands, row_send)

        @pl.when(rank == last)
        def _():
            settle(c, far * half_bands, late_send)

        @pl.when(rank > 0)
        def _():
            settle(c, far * half_bands, help_send)

    @pl.loop(0, chunks * pieces)
    def _(p):
        @pl.when(rank < last)
        def _():
            chain(firsts, p, first_send, first_recv).wait_send()

        @pl.when((rank > 0) & (rank < last))
        def _():
            chain(seconds, p, second_send, second_recv).wait_send()

    @pl.loop(0, pairs)
    def _(k):
        point_copy(me, partner, pass_send.at[k]).wait_send()


def on_device(grid_count, pt_count, orbitals, point_index, factor_panels):
    own_bands, grid_rows = orbitals.shape
    rows_here = grid_rows // grid_count
    panel = point_index.shape[0]
    chunks = rows_here // LANES
    bands = own_bands * grid_count
    vmem = pl.BlockSpec(memory_space=pltpu.VMEM)
    hbm = pl.BlockSpec(memory_space=pl.ANY)
    dma = pltpu.SemaphoreType.DMA
    return pl.pallas_call(
        functools.partial(kernel, grid_count, pt_count),
        out_shape=jax.ShapeDtypeStruct((rows_here, panel), F32),
        in_specs=[vmem, hbm, hbm],
        out_specs=vmem,
        scratch_shapes=[
            pltpu.VMEM((own_bands, grid_rows), BF16),
            pltpu.VMEM(factor_panels.shape, F32),
            pltpu.VMEM((chunks, 2, bands // 2, LANES), BF16),
            pltpu.VMEM((2, bands // 2, panel), BF16),
            pltpu.VMEM((own_bands, panel), F32),
            pltpu.VMEM((panel, panel), F32),
            pltpu.VMEM((panel, panel), F32),
            pltpu.VMEM((panel, panel), BF16),
            pltpu.VMEM((panel, panel), BF16),
            pltpu.VMEM((panel, panel), BF16),
            pltpu.VMEM((panel, panel), BF16),
            pltpu.VMEM((rows_here // PIECE, PIECE, panel), BF16),
            pltpu.VMEM((rows_here // PIECE, PIECE, panel), BF16),
            dma((2,)),
            *[dma((chunks,))] * 7,
            dma((grid_count // 2,)),
            dma((grid_count,)),
            dma((grid_count // 2,)),
            *[dma((rows_here // PIECE,))] * 4,
        ],
        compiler_params=pltpu.CompilerParams(
            collective_id=0, has_side_effects=True, vmem_limit_bytes=56 * 1024 * 1024
        ),
    )(point_index.reshape(1, panel), orbitals, factor_panels)


def solution(mesh):
    in_specs = (P("grid", None), P("pt"), P("pt", None))
    out_specs = P("grid", "pt")
    body = functools.partial(on_device, mesh.shape["grid"], mesh.shape["pt"])
    return jax.shard_map(
        body, mesh=mesh, in_specs=in_specs, out_specs=out_specs, check_vma=False
    )
```

profile of v0, /device:TPU:24, one launch (start us, length us, event | category | flops | bytes accessed | tf_op | source)
XLA Modules:
  0.0 57.1 jit_solution(7172684985505090330)
XLA Ops:
  0.0 54.8 %shard_map.37 = f32[512,512]{1,0:T(8,128)} custom-call(s32[1,512]{1,0:T(1,128)} %bitcast.1, bf16[256,4096]{1,0:T(8,128)(2,1)} %orb.1, f32[512,1024]{1,0:T(8,128)} %fac.1), custom_call_target="tpu_custom_call" | custom-call | tf_op jit(solution)/shard_map/pallas_call | solution.py:390
  54.8 2.3 %copy.5 = f32[512,512]{1,0:T(8,128)} copy(f32[512,512]{1,0:T(8,128)} %shard_map.37) | data formatting | bytes 2097152
where the time goes:
time: 57.2 us; the launch traced here: 57.1 us
  Pallas kernels  54.8 us (96%)
  local copies, waits for them, and re-layouts  2.26 us (4%)
    pallas_call x1, Pallas kernels, on_device(): pl.pallas_call(functools.partial(kernel, grid_count, pt_count), out_shape...  54.8 us
    unnamed x1, local copies, waits for them, and re-layouts  2.26 us

commit v1 on v0

v1 whole, which is shorter than its diff:
```python
import contextlib
import functools
import jax
import jax.numpy as jnp
from jax import lax
from jax.experimental import pallas as pl
from jax.experimental.pallas import tpu as pltpu
from jax.sharding import PartitionSpec as P

MESH = pl.DeviceIdType.MESH
F32, BF16, I16, I32 = jnp.float32, jnp.bfloat16, jnp.int16, jnp.int32
LANES = 128
PIECE = 32
TOP = 32000.0


def scope(_):
    return contextlib.nullcontext()


def split(value):
    high = value.astype(BF16)
    return high, (value - high.astype(F32)).astype(BF16)


def dot(a, b):
    return jnp.dot(a, b, preferred_element_type=F32)


def exact_dot(a, b):
    return jnp.dot(a, b, preferred_element_type=F32, precision=lax.Precision.HIGHEST)


def over_bands(a, b):
    return lax.dot_general(a, b, (((0,), (0,)), ((), ())), preferred_element_type=F32)


def each(low, high, body):
    if high - low <= 4:
        for i in range(low, high):
            body(i)
    else:
        pl.loop(low, high)(body)


def invert_lower(low, inv):
    size = low.shape[0]
    blocks = size // LANES
    row = lax.broadcasted_iota(jnp.int32, (LANES, LANES), 0)
    col = lax.broadcasted_iota(jnp.int32, (LANES, LANES), 1)
    tiles, parts = [], []
    for i in range(blocks):
        at = slice(i * LANES, (i + 1) * LANES)
        tile = low[at, at]
        tiles.append(tile)
        parts.append(jnp.where(row == col, 1.0 / jnp.where(row == col, tile, 1.0), 0.0))
    half = 1
    level = 0
    while half < LANES:
        rb, cb = row >> level, col >> level
        mask = ((rb >> 1) == (cb >> 1)) & (rb > cb)
        mids = [exact_dot(jnp.where(mask, tiles[i], 0.0), parts[i]) for i in range(blocks)]
        parts = [parts[i] - exact_dot(parts[i], mids[i]) for i in range(blocks)]
        half *= 2
        level += 1
    inv[...] = jnp.zeros_like(inv)
    for i in range(blocks):
        at = slice(i * LANES, (i + 1) * LANES)
        inv[at, at] = parts[i]
    width = LANES
    while width < size:
        for start in range(0, size, 2 * width):
            top = slice(start, start + width)
            bottom = slice(start + width, start + 2 * width)
            mid = exact_dot(low[bottom, top], inv[top, top])
            inv[bottom, top] = -exact_dot(inv[bottom, bottom], mid)
        width *= 2


def kernel(
    grid_count, pt_count, index, orb, fac, out,
    index_v, orb_v, fac_v, near, points, gathered, norms, scales, sent, came,
    low, inv, a_high, a_low, b_high, b_low, firsts, seconds,
    load_sem, index_sem, fac_sem, near_send, near_recv, point_send, point_recv, norm_send, norm_recv,
    part_send, part_recv, first_send, first_recv, second_send, second_recv,
):
    me = lax.axis_index("grid")
    rank = lax.axis_index("pt")
    own_bands, grid_rows = orb.shape
    chunks = near.shape[0]
    panel = index.shape[1]
    piece = firsts.shape[1]
    pieces = LANES // piece
    rows_here = chunks * LANES
    core = lax.rem(me, 2)
    chip = lax.div(me, 2)
    partner = me + 1 - 2 * core
    pairs = grid_count // 2
    last = pt_count - 1
    depth = min(1024, grid_rows)
    steps = grid_rows // depth

    def load(s):
        at = pl.ds(pl.multiple_of(s * depth, depth), depth)
        return pltpu.make_async_copy(orb.at[:, at], orb_v.at[:, at], load_sem.at[s])

    load_index = pltpu.make_async_copy(index, index_v, index_sem)
    load_fac = pltpu.make_async_copy(fac, fac_v, fac_sem)
    load_index.start()
    each(0, steps, lambda s: load(s).start())
    load_fac.start()

    barrier = pltpu.get_barrier_semaphore()

    @pl.loop(1, grid_count)
    def _(k):
        other = lax.rem(me + k, grid_count)
        pl.semaphore_signal(barrier, inc=1, device_id=(other, rank), device_id_type=MESH)

    @pl.when(rank > 0)
    def _():
        pl.semaphore_signal(barrier, inc=1, device_id=(me, rank - 1), device_id_type=MESH)

    @pl.when(rank < last)
    def _():
        pl.semaphore_signal(barrier, inc=1, device_id=(me, rank + 1), device_id_type=MESH)

    with scope("t_load"):
        load_index.wait()
        load(0).wait()

    with scope("t_gather"):
        gathered[...] = jnp.zeros_like(gathered)
        norms[me] = jnp.zeros(norms.shape[1:], F32)

        @pl.loop(0, steps)
        def _(s):
            @pl.when(s > 0)
            def _():
                load(s).wait()

            part = orb_v[:, pl.ds(pl.multiple_of(s * depth, depth), depth)]
            ids = lax.broadcasted_iota(jnp.int32, (depth, panel), 0) + s * depth
            hot = jnp.where(ids == index_v[...], 1.0, 0.0).astype(BF16)
            gathered[...] += dot(part, hot)
            wide = part.astype(F32)
            size = jnp.max(jnp.sum(wide * wide, axis=0, keepdims=True), axis=1, keepdims=True)
            norms[me] = jnp.maximum(norms[me], size)

        points[core] = gathered[...].astype(BF16)

    at_end = (rank == 0) | (rank == last)

    with scope("t_barrier"):
        @pl.when(at_end)
        def _():
            pl.semaphore_wait(barrier, grid_count)

        @pl.when(jnp.logical_not(at_end))
        def _():
            pl.semaphore_wait(barrier, grid_count + 1)

    def norm_copy(g, target):
        return pltpu.make_async_remote_copy(
            src_ref=norms.at[g],
            dst_ref=norms.at[g],
            send_sem=norm_send.at[target],
            recv_sem=norm_recv.at[g],
            device_id=(target, rank),
            device_id_type=MESH,
        )

    def point_copy(slot):
        return pltpu.make_async_remote_copy(
            src_ref=points.at[slot],
            dst_ref=points.at[slot],
            send_sem=point_send,
            recv_sem=point_recv,
            device_id=(partner, rank),
            device_id_type=MESH,
        )

    def near_copy(q, c):
        start = (2 * c + 1 - core) * rows_here + q * LANES
        return pltpu.make_async_remote_copy(
            src_ref=orb_v.at[:, pl.ds(pl.multiple_of(start, LANES), LANES)],
            dst_ref=near.at[q, :, pl.ds(pl.multiple_of(c * LANES, LANES), LANES)],
            send_sem=near_send.at[q],
            recv_sem=near_recv.at[q],
            device_id=(partner, rank),
            device_id_type=MESH,
        )

    norm_copy(me, partner).start()
    point_copy(core).start()
    for q in range(chunks):
        each(0, pairs, lambda c: near_copy(q, c).start())

    @pl.loop(1, grid_count)
    def _(k):
        other = lax.rem(me + k, grid_count)

        @pl.when(other != partner)
        def _():
            norm_copy(me, other).start()

    with scope("t_invert"):
        load_fac.wait()

        @pl.when(rank < 2)
        def _():
            start = pl.multiple_of(rank * panel, panel)
            low[...] = fac_v[:, pl.ds(start, panel)]
            invert_lower(low, inv)

        @pl.when(rank > 0)
        def _():
            a_high[...], a_low[...] = split(fac_v[:, 0:panel].T)

        @pl.when(rank == 0)
        def _():
            a_high[...], a_low[...] = split(inv[...].T)

        @pl.when(rank > 1)
        def _():
            b_high[...], b_low[...] = split(fac_v[:, panel : 2 * panel].T)

        @pl.when(rank == 1)
        def _():
            b_high[...], b_low[...] = split(inv[...].T)

    def bound(c):
        both = norms[2 * c, 0:1, 0:1] + norms[2 * c + 1, 0:1, 0:1]
        return jnp.broadcast_to(jnp.maximum(both, 1e-30), scales.shape[1:])

    with scope("t_partner"):
        norm_copy(partner, me).wait_recv()
        scales[0] = TOP / bound(chip)
        point_copy(1 - core).wait_recv()

    def part_copy(p, i):
        return pltpu.make_async_remote_copy(
            src_ref=sent.at[p, i - 1],
            dst_ref=came.at[p, i - 1],
            send_sem=part_send.at[p],
            recv_sem=part_recv.at[p],
            device_id=(2 * lax.rem(chip + i, pairs) + core, rank),
            device_id_type=MESH,
        )

    def sums(q, c):
        start = (2 * c + core) * rows_here + q * LANES
        mine = orb_v[:, pl.ds(pl.multiple_of(start, LANES), LANES)]
        other = near[q, :, pl.ds(pl.multiple_of(c * LANES, LANES), LANES)]
        return over_bands(mine, points[core]) + over_bands(other, points[1 - core])

    for q in range(chunks):
        with scope("t_near"):
            part = near.at[q]
            pltpu.make_async_copy(part, part, near_recv.at[q]).wait()
        with scope("t_parts"):

            def for_other(i):
                value = sums(q, lax.rem(chip + i, pairs)) * scales[0, 0:1, :]
                coded = jnp.round(value).astype(I32).astype(I16)
                for j in range(pieces):
                    sent[q * pieces + j, i - 1] = coded[j * piece : (j + 1) * piece]

            each(1, pairs, for_other)
            for j in range(pieces):
                each(1, pairs, lambda i: part_copy(q * pieces + j, i).start())
            out[q * LANES : (q + 1) * LANES, :] = sums(q, chip)

    with scope("t_norms"):
        @pl.loop(1, grid_count)
        def _(k):
            other = lax.rem(me + k, grid_count)

            @pl.when(other != partner)
            def _():
                norm_copy(other, me).wait_recv()

        def source_scale(i):
            scales[i] = bound(lax.rem(chip + pairs - i, pairs)) * (1.0 / TOP)

        each(1, pairs, source_scale)

    def chain(buf, p, send_sem, recv_sem):
        return pltpu.make_async_remote_copy(
            src_ref=buf.at[p],
            dst_ref=buf.at[p],
            send_sem=send_sem.at[p],
            recv_sem=recv_sem.at[p],
            device_id=(me, rank + 1),
            device_id_type=MESH,
        )

    def solve(value, high, low_part):
        value_high, value_low = split(value)
        return dot(value_high, high[...]) + (dot(value_high, low_part[...]) + dot(value_low, high[...]))

    def apply(value, high, low_part):
        return dot(value, high[...]) + dot(value, low_part[...])

    @pl.loop(0, chunks * pieces)
    def _(p):
        here = pl.ds(pl.multiple_of(p * piece, piece), piece)
        with scope("t_came"):
            part = came.at[p]
            pltpu.make_async_copy(part, part, part_recv.at[p]).wait()
        with scope("t_sum"):

            def add(i):
                out[here, :] += came[p, i - 1].astype(I32).astype(F32) * scales[i, 0:1, :]

            each(1, pairs, add)
            out[here, :] = out[here, :] * out[here, :]

        with scope("t_first"):
            @pl.when(rank == 0)
            def _():
                first = solve(out[here, :], a_high, a_low)
                out[here, :] = first
                firsts[p] = first.astype(BF16)

            @pl.when(rank > 0)
            def _():
                chain(firsts, p, first_send, first_recv).wait_recv()

            @pl.when(rank < last)
            def _():
                chain(firsts, p, first_send, first_recv).start()

        with scope("t_second"):
            @pl.when(rank > 0)
            def _():
                out[here, :] -= apply(firsts[p], a_high, a_low)

            @pl.when(rank == 1)
            def _():
                second = solve(out[here, :], b_high, b_low)
                out[here, :] = second
                seconds[p] = second.astype(BF16)

            @pl.when(rank > 1)
            def _():
                chain(seconds, p, second_send, second_recv).wait_recv()

            @pl.when((rank > 0) & (rank < last))
            def _():
                chain(seconds, p, second_send, second_recv).start()

        with scope("t_last"):
            @pl.when(rank > 1)
            def _():
                out[here, :] -= apply(seconds[p], b_high, b_low)

    with scope("t_drain"):
        for q in range(chunks):
            part = near.at[q]
            pltpu.make_async_copy(part, part, near_send.at[q]).wait()
        point_copy(core).wait_send()

        @pl.loop(1, grid_count)
        def _(k):
            norm_copy(me, lax.rem(me + k, grid_count)).wait_send()

        @pl.loop(0, chunks * pieces)
        def _(p):
            part = sent.at[p]
            pltpu.make_async_copy(part, part, part_send.at[p]).wait()

            @pl.when(rank < last)
            def _():
                chain(firsts, p, first_send, first_recv).wait_send()

            @pl.when((rank > 0) & (rank < last))
            def _():
                chain(seconds, p, second_send, second_recv).wait_send()


def on_device(grid_count, pt_count, orbitals, point_index, factor_panels):
    own_bands, grid_rows = orbitals.shape
    rows_here = grid_rows // grid_count
    panel = point_index.shape[0]
    chunks = rows_here // LANES
    pairs = grid_count // 2
    pieces = rows_here // PIECE
    hbm = pl.BlockSpec(memory_space=pl.ANY)
    dma = pltpu.SemaphoreType.DMA
    square = [pltpu.VMEM((panel, panel), t) for t in (F32, F32, BF16, BF16, BF16, BF16)]
    scratch = [
        pltpu.VMEM((1, panel), I32),
        pltpu.VMEM((own_bands, grid_rows), BF16),
        pltpu.VMEM(factor_panels.shape, F32),
        pltpu.VMEM((chunks, own_bands, pairs * LANES), BF16),
        pltpu.VMEM((2, own_bands, panel), BF16),
        pltpu.VMEM((own_bands, panel), F32),
        pltpu.VMEM((grid_count, 8, LANES), F32),
        pltpu.VMEM((pairs, 8, panel), F32),
        pltpu.VMEM((pieces, pairs - 1, PIECE, panel), I16),
        pltpu.VMEM((pieces, pairs - 1, PIECE, panel), I16),
        *square,
        pltpu.VMEM((pieces, PIECE, panel), BF16),
        pltpu.VMEM((pieces, PIECE, panel), BF16),
    ]
    used = sum(s.dtype.itemsize * functools.reduce(lambda a, b: a * b, s.shape) for s in scratch)
    sems = [
        dma((grid_rows // min(1024, grid_rows),)),
        dma, dma,
        dma((chunks,)), dma((chunks,)),
        dma, dma,
        dma((grid_count,)), dma((grid_count,)),
        *[dma((pieces,))] * 6,
    ]
    args = [point_index.reshape(1, panel), orbitals, factor_panels]
    return pl.pallas_call(
        functools.partial(kernel, grid_count, pt_count),
        out_shape=jax.ShapeDtypeStruct((rows_here, panel), F32),
        in_specs=[hbm] * 3,
        out_specs=pl.BlockSpec(memory_space=pltpu.VMEM),
        scratch_shapes=scratch + sems,
        compiler_params=pltpu.CompilerParams(
            collective_id=0, has_side_effects=True, vmem_limit_bytes=used + 8 * 1024 * 1024
        ),
    )(*[pltpu.with_memory_space_constraint(a, pltpu.HBM) for a in args])


def solution(mesh):
    in_specs = (P("grid", None), P("pt"), P("pt", None))
    out_specs = P("grid", "pt")
    body = functools.partial(on_device, mesh.shape["grid"], mesh.shape["pt"])
    return jax.shard_map(
        body, mesh=mesh, in_specs=in_specs, out_specs=out_specs, check_vma=False
    )
```

time: 57.2 us -> 45.5 us (0.80)
  Pallas kernels: 54.8 us -> 44.3 us
  local copies, waits for them, and re-layouts: 2.26 us -> 0.97 us
    pallas_call x1, Pallas kernels: 54.8 us -> 44.3 us  [on_device(): pl.pallas_call(functools.partial(kernel, grid_count, pt_count), out_shape...]
    unnamed x1, local copies, waits for them, and re-layouts: 2.26 us -> 0.97 us
where the time goes in v1:
time: 45.5 us; the launch traced here: 45.3 us
  Pallas kernels  44.3 us (97%)
  local copies, waits for them, and re-layouts  0.97 us (2%)
    pallas_call x1, Pallas kernels, on_device(): pl.pallas_call(functools.partial(kernel, grid_count, pt_count), out_shape...  44.3 us
    unnamed x1, local copies, waits for them, and re-layouts  0.97 us

profile of v1, /device:TPU:24, one launch (start us, length us, event | category | flops | bytes accessed | tf_op | source)
XLA Modules:
  0.0 45.3 jit_solution(16937555295671370079)
XLA Ops:
  0.0 44.3 %shard_map.37 = f32[512,512]{1,0:T(8,128)S(1)} custom-call(s32[1,512]{1,0:T(1,128)} %bitcast.1, bf16[256,4096]{1,0:T(8,128)(2,1)} %orb.1, f32[512,1024]{1,0:T(8,128)} %fac.1), custom_call_target="tpu_custom_call" | custom-call | tf_op jit(solution)/shard_map/pallas_call | solution.py:417
  44.3 1.0 %copy.5 = f32[512,512]{1,0:T(8,128)} copy(f32[512,512]{1,0:T(8,128)S(1)} %shard_map.37) | data formatting | bytes 2097152

commit v2 on v1

--- a/solution.py
+++ b/solution.py
@@ -27,8 +27,17 @@
     return jnp.dot(a, b, preferred_element_type=F32)
 
 
-def exact_dot(a, b):
-    return jnp.dot(a, b, preferred_element_type=F32, precision=lax.Precision.HIGHEST)
+def fine_dot(a, b):
+    size = b.shape[1]
+    a_high, a_low = split(a)
+    b_high, b_low = split(b)
+    if size > LANES:
+        return dot(a_high, b_high) + (dot(a_high, b_low) + dot(a_low, b_high))
+    left = jnp.concatenate([a_high, a_low], axis=1)
+    top = jnp.concatenate([b_high, b_low], axis=1)
+    bottom = jnp.concatenate([b_high, jnp.zeros_like(b_high)], axis=1)
+    both = dot(left, jnp.concatenate([top, bottom], axis=0))
+    return both[:, :size] + both[:, size:]
 
 
 def over_bands(a, b):
@@ -53,14 +62,17 @@
         at = slice(i * LANES, (i + 1) * LANES)
         tile = low[at, at]
         tiles.append(tile)
-        parts.append(jnp.where(row == col, 1.0 / jnp.where(row == col, tile, 1.0), 0.0))
-    half = 1
-    level = 0
+        part = jnp.where(row == col, 1.0 / jnp.where(row == col, tile, 1.0), 0.0)
+        below = jnp.where((row >> 1 == col >> 1) & (row > col), tile, 0.0)
+        down, across = jnp.sum(part, axis=1, keepdims=True), jnp.sum(part, axis=0, keepdims=True)
+        parts.append(part - below * down * across)
+    half = 2
+    level = 1
     while half < LANES:
         rb, cb = row >> level, col >> level
         mask = ((rb >> 1) == (cb >> 1)) & (rb > cb)
-        mids = [exact_dot(jnp.where(mask, tiles[i], 0.0), parts[i]) for i in range(blocks)]
-        parts = [parts[i] - exact_dot(parts[i], mids[i]) for i in range(blocks)]
+        mids = [fine_dot(jnp.where(mask, tiles[i], 0.0), parts[i]) for i in range(blocks)]
+        parts = [parts[i] - fine_dot(parts[i], mids[i]) for i in range(blocks)]
         half *= 2
         level += 1
     inv[...] = jnp.zeros_like(inv)
@@ -72,8 +84,8 @@
         for start in range(0, size, 2 * width):
             top = slice(start, start + width)
             bottom = slice(start + width, start + 2 * width)
-            mid = exact_dot(low[bottom, top], inv[top, top])
-            inv[bottom, top] = -exact_dot(inv[bottom, bottom], mid)
+            mid = fine_dot(low[bottom, top], inv[top, top])
+            inv[bottom, top] = -fine_dot(inv[bottom, bottom], mid)
         width *= 2
 
 
@@ -164,7 +176,7 @@
         return pltpu.make_async_remote_copy(
             src_ref=norms.at[g],
             dst_ref=norms.at[g],
-            send_sem=norm_send.at[target],
+            send_sem=norm_send,
             recv_sem=norm_recv.at[g],
             device_id=(target, rank),
             device_id_type=MESH,
@@ -185,7 +197,7 @@
         return pltpu.make_async_remote_copy(
             src_ref=orb_v.at[:, pl.ds(pl.multiple_of(start, LANES), LANES)],
             dst_ref=near.at[q, :, pl.ds(pl.multiple_of(c * LANES, LANES), LANES)],
-            send_sem=near_send.at[q],
+            send_sem=near_send,
             recv_sem=near_recv.at[q],
             device_id=(partner, rank),
             device_id_type=MESH,
@@ -204,31 +216,6 @@
         def _():
             norm_copy(me, other).start()
 
-    with scope("t_invert"):
-        load_fac.wait()
-
-        @pl.when(rank < 2)
-        def _():
-            start = pl.multiple_of(rank * panel, panel)
-            low[...] = fac_v[:, pl.ds(start, panel)]
-            invert_lower(low, inv)
-
-        @pl.when(rank > 0)
-        def _():
-            a_high[...], a_low[...] = split(fac_v[:, 0:panel].T)
-
-        @pl.when(rank == 0)
-        def _():
-            a_high[...], a_low[...] = split(inv[...].T)
-
-        @pl.when(rank > 1)
-        def _():
-            b_high[...], b_low[...] = split(fac_v[:, panel : 2 * panel].T)
-
-        @pl.when(rank == 1)
-        def _():
-            b_high[...], b_low[...] = split(inv[...].T)
-
     def bound(c):
         both = norms[2 * c, 0:1, 0:1] + norms[2 * c + 1, 0:1, 0:1]
         return jnp.broadcast_to(jnp.maximum(both, 1e-30), scales.shape[1:])
@@ -242,11 +229,14 @@
         return pltpu.make_async_remote_copy(
             src_ref=sent.at[p, i - 1],
             dst_ref=came.at[p, i - 1],
-            send_sem=part_send.at[p],
+            send_sem=part_send,
             recv_sem=part_recv.at[p],
             device_id=(2 * lax.rem(chip + i, pairs) + core, rank),
             device_id_type=MESH,
         )
+
+    def rows_of(q):
+        return pl.ds(pl.multiple_of(q * LANES, LANES), LANES)
 
     def sums(q, c):
         start = (2 * c + core) * rows_here + q * LANES
@@ -254,7 +244,7 @@
         other = near[q, :, pl.ds(pl.multiple_of(c * LANES, LANES), LANES)]
         return over_bands(mine, points[core]) + over_bands(other, points[1 - core])
 
-    for q in range(chunks):
+    def send_parts(q):
         with scope("t_near"):
             part = near.at[q]
             pltpu.make_async_copy(part, part, near_recv.at[q]).wait()
@@ -269,7 +259,34 @@
             each(1, pairs, for_other)
             for j in range(pieces):
                 each(1, pairs, lambda i: part_copy(q * pieces + j, i).start())
-            out[q * LANES : (q + 1) * LANES, :] = sums(q, chip)
+            out[rows_of(q), :] = sums(q, chip)
+
+    send_parts(0)
+
+    with scope("t_invert"):
+        load_fac.wait()
+
+        @pl.when(rank < 2)
+        def _():
+            start = pl.multiple_of(rank * panel, panel)
+            low[...] = fac_v[:, pl.ds(start, panel)]
+            invert_lower(low, inv)
+
+        @pl.when(rank > 0)
+        def _():
+            a_high[...], a_low[...] = split(fac_v[:, 0:panel].T)
+
+        @pl.when(rank == 0)
+        def _():
+            a_high[...], a_low[...] = split(inv[...].T)
+
+        @pl.when(rank > 1)
+        def _():
+            b_high[...], b_low[...] = split(fac_v[:, panel : 2 * panel].T)
+
+        @pl.when(rank == 1)
+        def _():
+            b_high[...], b_low[...] = split(inv[...].T)
 
     with scope("t_norms"):
         @pl.loop(1, grid_count)
@@ -285,19 +302,32 @@
 
         each(1, pairs, source_scale)
 
+    if chunks > 1:
+        send_parts(1)
+
     def chain(buf, p, send_sem, recv_sem):
         return pltpu.make_async_remote_copy(
             src_ref=buf.at[p],
             dst_ref=buf.at[p],
-            send_sem=send_sem.at[p],
+            send_sem=send_sem,
             recv_sem=recv_sem.at[p],
             device_id=(me, rank + 1),
             device_id_type=MESH,
         )
 
+    half = panel // 2
+
     def solve(value, high, low_part):
         value_high, value_low = split(value)
-        return dot(value_high, high[...]) + (dot(value_high, low_part[...]) + dot(value_low, high[...]))
+        both = jnp.concatenate([value_high, value_low], axis=0)
+
+        def columns(k, at):
+            wide = dot(both[:, k], high[k, at])
+            return wide[:piece] + (dot(value_high[:, k], low_part[k, at]) + wide[piece:])
+
+        left = columns(slice(0, half), slice(0, half))
+        right = columns(slice(0, panel), slice(half, panel))
+        return jnp.concatenate([left, right], axis=1)
 
     def apply(value, high, low_part):
         return dot(value, high[...]) + dot(value, low_part[...])
@@ -355,28 +385,26 @@
             def _():
                 out[here, :] -= apply(seconds[p], b_high, b_low)
 
+        @pl.when((lax.rem(p, pieces) == 1) & (p < (chunks - 2) * pieces))
+        def _():
+            send_parts(lax.div(p, pieces) + 2)
+
+    def sent_all(part, sem):
+        pltpu.make_async_copy(part, part, sem).wait()
+
     with scope("t_drain"):
-        for q in range(chunks):
-            part = near.at[q]
-            pltpu.make_async_copy(part, part, near_send.at[q]).wait()
+        sent_all(near, near_send)
+        sent_all(sent, part_send)
+        sent_all(norms.at[pl.ds(0, grid_count - 1)], norm_send)
         point_copy(core).wait_send()
 
-        @pl.loop(1, grid_count)
-        def _(k):
-            norm_copy(me, lax.rem(me + k, grid_count)).wait_send()
-
-        @pl.loop(0, chunks * pieces)
-        def _(p):
-            part = sent.at[p]
-            pltpu.make_async_copy(part, part, part_send.at[p]).wait()
-
-            @pl.when(rank < last)
-            def _():
-                chain(firsts, p, first_send, first_recv).wait_send()
-
-            @pl.when((rank > 0) & (rank < last))
-            def _():
-                chain(seconds, p, second_send, second_recv).wait_send()
+        @pl.when(rank < last)
+        def _():
+            sent_all(firsts, first_send)
+
+        @pl.when((rank > 0) & (rank < last))
+        def _():
+            sent_all(seconds, second_send)
 
 
 def on_device(grid_count, pt_count, orbitals, point_index, factor_panels):
@@ -408,10 +436,10 @@
     sems = [
         dma((grid_rows // min(1024, grid_rows),)),
         dma, dma,
-        dma((chunks,)), dma((chunks,)),
+        dma, dma((chunks,)),
         dma, dma,
-        dma((grid_count,)), dma((grid_count,)),
-        *[dma((pieces,))] * 6,
+        dma, dma((grid_count,)),
+        *[dma, dma((pieces,))] * 3,
     ]
     args = [point_index.reshape(1, panel), orbitals, factor_panels]
     return pl.pallas_call(

time: 45.5 us -> 41.1 us (0.903); the launches traced: 45.3 us -> 40.3 us
  Pallas kernels: 44.3 us -> 39.4 us
    pallas_call x1, Pallas kernels: 44.3 us -> 39.4 us  [on_device(): pl.pallas_call(functools.partial(kernel, grid_count, pt_count), out_shape...]
where the time goes in v2:
time: 41.1 us; the launch traced here: 40.3 us
  Pallas kernels  39.4 us (96%)
  local copies, waits for them, and re-layouts  0.97 us (2%)
    pallas_call x1, Pallas kernels, on_device(): pl.pallas_call(functools.partial(kernel, grid_count, pt_count), out_shape...  39.4 us
    unnamed x1, local copies, waits for them, and re-layouts  0.97 us

profile of v2, /device:TPU:24, one launch (start us, length us, event | category | flops | bytes accessed | tf_op | source)
XLA Modules:
  0.0 40.3 jit_solution(2336059017374175962)
XLA Ops:
  0.0 39.4 %shard_map.37 = f32[512,512]{1,0:T(8,128)S(1)} custom-call(s32[1,512]{1,0:T(1,128)} %bitcast.1, bf16[256,4096]{1,0:T(8,128)(2,1)} %orb.1, f32[512,1024]{1,0:T(8,128)} %fac.1), custom_call_target="tpu_custom_call" | custom-call | tf_op jit(solution)/shard_map/pallas_call | solution.py:445
  39.4 1.0 %copy.5 = f32[512,512]{1,0:T(8,128)} copy(f32[512,512]{1,0:T(8,128)S(1)} %shard_map.37) | data formatting | bytes 2097152

commit v3 on v2

v3 whole, which is shorter than its diff:
```python
import contextlib
import functools
import jax
import jax.numpy as jnp
from jax import lax
from jax.experimental import pallas as pl
from jax.experimental.pallas import tpu as pltpu
from jax.sharding import PartitionSpec as P

MESH = pl.DeviceIdType.MESH
F32, BF16, I16, I32 = jnp.float32, jnp.bfloat16, jnp.int16, jnp.int32
LANES = 128
PIECE = 32
SMALL = 16
BLOCK = 256
HELPER = 3
TOP = 32000.0


def scope(_):
    return contextlib.nullcontext()


def split(value):
    high = value.astype(BF16)
    return high, (value - high.astype(F32)).astype(BF16)


def dot(a, b):
    return jnp.dot(a, b, preferred_element_type=F32)


def fine_dot(a, b):
    size = b.shape[1]
    a_high, a_low = split(a)
    b_high, b_low = split(b)
    if size > LANES:
        return dot(a_high, b_high) + (dot(a_high, b_low) + dot(a_low, b_high))
    left = jnp.concatenate([a_high, a_low], axis=1)
    top = jnp.concatenate([b_high, b_low], axis=1)
    bottom = jnp.concatenate([b_high, jnp.zeros_like(b_high)], axis=1)
    both = dot(left, jnp.concatenate([top, bottom], axis=0))
    return both[:, :size] + both[:, size:]


def over_bands(a, b):
    return lax.dot_general(a, b, (((0,), (0,)), ((), ())), preferred_element_type=F32)


def each(low, high, body):
    if high - low <= 4:
        for i in range(low, high):
            body(i)
    else:
        pl.loop(low, high)(body)


def invert_lower(low, inv):
    size = low.shape[0]
    blocks = size // LANES
    row = lax.broadcasted_iota(jnp.int32, (LANES, LANES), 0)
    col = lax.broadcasted_iota(jnp.int32, (LANES, LANES), 1)
    tiles, parts = [], []
    for i in range(blocks):
        at = slice(i * LANES, (i + 1) * LANES)
        tile = low[at, at]
        tiles.append(tile)
        part = jnp.where(row == col, 1.0 / jnp.where(row == col, tile, 1.0), 0.0)
        below = jnp.where((row >> 1 == col >> 1) & (row > col), tile, 0.0)
        down, across = jnp.sum(part, axis=1, keepdims=True), jnp.sum(part, axis=0, keepdims=True)
        parts.append(part - below * down * across)
    half = 2
    level = 1
    while half < LANES:
        rb, cb = row >> level, col >> level
        mask = ((rb >> 1) == (cb >> 1)) & (rb > cb)
        mids = [fine_dot(jnp.where(mask, tiles[i], 0.0), parts[i]) for i in range(blocks)]
        parts = [parts[i] - fine_dot(parts[i], mids[i]) for i in range(blocks)]
        half *= 2
        level += 1
    inv[...] = jnp.zeros_like(inv)
    for i in range(blocks):
        at = slice(i * LANES, (i + 1) * LANES)
        inv[at, at] = parts[i]
    width = LANES
    while width < size:
        for start in range(0, size, 2 * width):
            top = slice(start, start + width)
            bottom = slice(start + width, start + 2 * width)
            mid = fine_dot(low[bottom, top], inv[top, top])
            inv[bottom, top] = -fine_dot(inv[bottom, bottom], mid)
        width *= 2


def kernel(
    grid_count, pt_count, index, orb, fac, out,
    index_v, orb_v, fac_v, near, points, gathered, ramp, early, norms, scales, sent, came,
    low, inv, a_high, a_low, b_high, b_low, firsts, seconds,
    lead_index, lead_points, lead_sent, lead_came, lead_sums, c_high, c_low,
    load_sem, index_sem, fac_sem, near_send, near_recv, point_send, point_recv, norm_send, norm_recv,
    part_send, part_recv, first_send, first_recv, second_send, second_recv,
    give_send, index_recv, low_recv, swap_send, swap_recv, lead_point_send, lead_point_recv,
    lead_part_send, lead_part_recv, sum_send, sum_recv,
):
    me = lax.axis_index("grid")
    rank = lax.axis_index("pt")
    own_bands, grid_rows = orb.shape
    chunks = near.shape[0]
    panel = index.shape[1]
    pieces = LANES // PIECE
    rows_here = chunks * LANES
    core = lax.rem(me, 2)
    chip = lax.div(me, 2)
    partner = me + 1 - 2 * core
    pairs = grid_count // 2
    last = pt_count - 1
    depth = min(1024, grid_rows)
    steps = grid_rows // depth
    blocks = depth // BLOCK
    smalls = PIECE // SMALL
    wide = rows_here // PIECE
    helped = rows_here - LANES
    is_helper = rank == HELPER

    def load(s):
        at = pl.ds(pl.multiple_of(s * depth, depth), depth)
        return pltpu.make_async_copy(orb.at[:, at], orb_v.at[:, at], load_sem.at[s])

    load_index = pltpu.make_async_copy(index, index_v, index_sem)
    load_fac = pltpu.make_async_copy(fac, fac_v, fac_sem)
    load_index.start()
    each(0, steps, lambda s: load(s).start())
    load_fac.start()

    barrier = pltpu.get_barrier_semaphore()

    def greet(g, r):
        pl.semaphore_signal(barrier, inc=1, device_id=(g, r), device_id_type=MESH)

    @pl.loop(1, grid_count)
    def _(k):
        greet(lax.rem(me + k, grid_count), rank)

    @pl.when(rank > 0)
    def _():
        greet(me, rank - 1)

    @pl.when(rank < last)
    def _():
        greet(me, rank + 1)

    @pl.when(rank < 2)
    def _():
        greet(me, HELPER)

    @pl.when(is_helper)
    def _():
        greet(me, 0)
        greet(me, 1)

    steps_of = lax.broadcasted_iota(I32, (BLOCK, panel), 0).astype(F32).astype(BF16)
    ramp[...] = steps_of.reshape(ramp.shape)

    with scope("t_load"):
        load_index.wait()
        load(0).wait()

    def gather(part, ids, s):
        hots = []
        for j in range(blocks):
            at = jnp.clip(ids[...] - (s * depth + j * BLOCK), -1, BLOCK).astype(F32)
            at = jnp.broadcast_to(at, (SMALL, panel)).astype(BF16)
            hot = jnp.where(ramp[...] == at[None], jnp.ones((), BF16), jnp.zeros((), BF16))
            hots.append(hot.reshape(BLOCK, panel))
        gathered[...] += dot(part, jnp.concatenate(hots, axis=0))

    def columns_of(s):
        return orb_v[:, pl.ds(pl.multiple_of(s * depth, depth), depth)]

    def gather_own(s):
        @pl.when(s > 0)
        def _():
            load(s).wait()

        part = columns_of(s)
        gather(part, index_v, s)
        value = part.astype(F32)
        size = jnp.max(jnp.sum(value * value, axis=0, keepdims=True), axis=1, keepdims=True)
        norms[me] = jnp.maximum(norms[me], size)

    with scope("t_gather"):
        gathered[...] = jnp.zeros_like(gathered)
        norms[me] = jnp.zeros(norms.shape[1:], F32)
        pl.loop(0, steps - 1)(gather_own)

    with scope("t_barrier"):
        near_ranks = (
            jnp.where(rank > 0, 1, 0) + jnp.where(rank < last, 1, 0)
            + jnp.where(rank < 2, 1, 0) + jnp.where(is_helper, 2, 0)
        )
        for count in range(1, 5):

            @pl.when(near_ranks == count)
            def _():
                pl.semaphore_wait(barrier, grid_count - 1 + count)

    def near_copy(q, c):
        start = (2 * c + 1 - core) * rows_here + q * LANES
        return pltpu.make_async_remote_copy(
            src_ref=orb.at[:, pl.ds(pl.multiple_of(start, LANES), LANES)],
            dst_ref=near.at[q, :, pl.ds(pl.multiple_of(c * LANES, LANES), LANES)],
            send_sem=near_send,
            recv_sem=near_recv.at[min(q, 1)],
            device_id=(partner, rank),
            device_id_type=MESH,
        )

    each(0, pairs, lambda c: near_copy(0, c).start())

    strips = panel // LANES

    def strip(ref, b):
        return ref.at[pl.ds(b * LANES, LANES), pl.ds(0, (b + 1) * LANES)]

    def for_half(half, body):
        @pl.when(core == half)
        def _():
            for b in range(strips // 2):
                if b % 2 == half:
                    body(b)
                    body(strips - 1 - b)

    half_rows = (strips // 4) * (strips + 1) * LANES * LANES // panel

    def copy_to(src, dst, send_sem, recv_sem, g, r):
        return pltpu.make_async_remote_copy(
            src_ref=src, dst_ref=dst, send_sem=send_sem, recv_sem=recv_sem,
            device_id=(g, r), device_id_type=MESH,
        )

    @pl.when(rank == 0)
    def _():
        copy_to(index_v, lead_index, give_send.at[0], index_recv, me, HELPER).start()
        for half in range(2):
            for_half(half, lambda b: copy_to(
                strip(fac, b), strip(low, b), give_send.at[1], low_recv, me, HELPER).start())

    with scope("t_gather2"):
        pl.loop(steps - 1, steps)(gather_own)
        points[core] = gathered[...].astype(BF16)

    def norm_copy(g, target, recv_sem):
        return copy_to(norms.at[g], norms.at[g], norm_send, recv_sem, target, rank)

    def point_copy(buf, slot, send_sem, recv_sem):
        return copy_to(buf.at[slot], buf.at[slot], send_sem, recv_sem, partner, rank)

    point_copy(points, core, point_send, point_recv).start()
    norm_copy(me, partner, norm_recv.at[0]).start()

    def bound(c):
        return norms[2 * c, 0:1, 0:1] + norms[2 * c + 1, 0:1, 0:1]

    def widen(value):
        return jnp.broadcast_to(jnp.maximum(value, 1e-30), scales.shape[1:])

    def peer(i):
        if pairs == 4:
            x, y = lax.rem(chip, 2), lax.div(chip, 2)
            return [chip, 3 - chip, chip + 2 - 4 * y, chip + 1 - 2 * x][i]
        return lax.rem(chip + i, pairs)

    def source(i):
        return peer(i) if pairs == 4 else lax.rem(chip + pairs - i, pairs)

    def rows_of(q):
        return pl.ds(pl.multiple_of(q * LANES, LANES), LANES)

    def rows_at(start, size):
        return pl.ds(pl.multiple_of(start, size), size)

    def own_sums(q, c, buf):
        start = (2 * c + core) * rows_here + q * LANES
        return over_bands(orb_v[:, pl.ds(pl.multiple_of(start, LANES), LANES)], buf[core])

    def near_sums(q, c, buf):
        part = near[q, :, pl.ds(pl.multiple_of(c * LANES, LANES), LANES)]
        return over_bands(part, buf[1 - core])

    def encode(value):
        return jnp.round(value * scales[0, 0:1, :]).astype(I32).astype(I16)

    def await_all(part, sem):
        pltpu.make_async_copy(part, part, sem).wait()

    ready = pairs <= early.shape[0]
    if ready:
        with scope("t_early"):
            for i in range(pairs):
                early[i] = own_sums(0, peer(i), points)

    for q in range(1, chunks):
        each(0, pairs, lambda c: near_copy(q, c).start())

    @pl.loop(1, grid_count)
    def _(k):
        other = lax.rem(me + k, grid_count)

        @pl.when(other != partner)
        def _():
            norm_copy(me, other, norm_recv.at[1]).start()

    with scope("t_partner"):
        norm_copy(partner, me, norm_recv.at[0]).wait_recv()
        scales[0] = TOP / widen(bound(chip))
        point_copy(points, 1 - core, point_send, point_recv).wait_recv()

    def part_copy(start, size, p, i):
        return copy_to(
            sent.at[i - 1, rows_at(start, size)], came.at[i - 1, rows_at(start, size)],
            part_send, part_recv.at[p], 2 * peer(i) + core, rank,
        )

    def send_rows(start, size, p):
        each(1, pairs, lambda i: part_copy(start, size, p, i).start())

    def send_parts(q, begun):
        def sums(i):
            c = peer(i)
            return (early[i] if begun else own_sums(q, c, points)) + near_sums(q, c, points)

        with scope("t_parts"):

            def for_other(i):
                sent[i - 1, rows_of(q)] = encode(sums(i))

            each(1, pairs, for_other)
            start, middle = q * LANES, q * pieces + smalls - 1
            if isinstance(q, int):
                for k in range(smalls):
                    send_rows(k * SMALL, SMALL, k)
            else:
                send_rows(start, PIECE, middle)
            for j in range(1, pieces - 1):
                send_rows(start + j * PIECE, PIECE, middle + j)
            at, p = start + (pieces - 1) * PIECE, middle + pieces - 1

            @pl.when(q < chunks - 1)
            def _():
                send_rows(at, PIECE, p)

            @pl.when(q == chunks - 1)
            def _():
                for k in range(smalls):
                    send_rows(at + k * SMALL, SMALL, p + k)

            out[rows_of(q), :] = sums(0)

    with scope("t_near"):
        await_all(near.at[0], near_recv.at[0])
    send_parts(0, ready)

    def lead_part_copy(i):
        return copy_to(
            lead_sent.at[i - 1], lead_came.at[i - 1], lead_part_send, lead_part_recv,
            2 * peer(i) + core, rank,
        )

    with scope("t_lead"):
        @pl.when(is_helper)
        def _():
            copy_to(index_v, lead_index, give_send.at[0], index_recv, me, rank).wait_recv()
            gathered[...] = jnp.zeros_like(gathered)

            @pl.loop(0, steps)
            def _(s):
                gather(columns_of(s), lead_index, s)

            lead_points[core] = gathered[...].astype(BF16)
            point_copy(lead_points, core, lead_point_send, lead_point_recv).start()

    with scope("t_near"):
        await_all(near.at[pl.ds(1, chunks - 1)], near_recv.at[1])

    with scope("t_lead"):
        @pl.when(is_helper)
        def _():
            point_copy(lead_points, 1 - core, lead_point_send, lead_point_recv).wait_recv()

            def lead_parts(i):
                c = peer(i)
                total = own_sums(chunks - 1, c, lead_points) + near_sums(chunks - 1, c, lead_points)
                lead_sent[i - 1] = encode(total)
                lead_part_copy(i).start()

            each(1, pairs, lead_parts)
            lead_sums[...] = own_sums(chunks - 1, chip, lead_points) + near_sums(chunks - 1, chip, lead_points)

    @pl.when(rank > 0)
    def _():
        @pl.loop(1, chunks)
        def _(q):
            send_parts(q, False)

    with scope("t_invert"):
        load_fac.wait()

        @pl.when(rank < 2)
        def _():
            start = pl.multiple_of(rank * panel, panel)
            low[...] = fac_v[:, pl.ds(start, panel)]

        @pl.when(is_helper)
        def _():
            half_low = low.at[pl.ds(0, half_rows)]
            await_all(half_low, low_recv)
            for half in range(2):
                for_half(half, lambda b: copy_to(
                    strip(low, b), strip(low, b), swap_send, swap_recv, partner, rank).start())
            await_all(half_low, swap_recv)

        @pl.when((rank < 2) | is_helper)
        def _():
            invert_lower(low, inv)

        @pl.when(rank > 0)
        def _():
            a_high[...], a_low[...] = split(fac_v[:, 0:panel].T)

        @pl.when(rank == 0)
        def _():
            a_high[...], a_low[...] = split(inv[...].T)

        @pl.when(rank > 1)
        def _():
            b_high[...], b_low[...] = split(fac_v[:, panel : 2 * panel].T)

        @pl.when(rank == 1)
        def _():
            b_high[...], b_low[...] = split(inv[...].T)

        @pl.when(is_helper)
        def _():
            c_high[...], c_low[...] = split(inv[...].T)

    def chain(buf, start, size, target, send_sem, recv_sem):
        part = buf.at[rows_at(start, size)]
        return copy_to(part, part, send_sem, recv_sem, me, target)

    half = panel // 2

    def solve(value, high, low_part):
        size = value.shape[0]
        value_high, value_low = split(value)
        both = jnp.concatenate([value_high, value_low], axis=0)

        def columns(k, at):
            total = dot(both[:, k], high[k, at])
            return total[:size] + (dot(value_high[:, k], low_part[k, at]) + total[size:])

        left = columns(slice(0, half), slice(0, half))
        right = columns(slice(0, panel), slice(half, panel))
        return jnp.concatenate([left, right], axis=1)

    def apply(value, high, low_part):
        return dot(value, high[...]) + dot(value, low_part[...])

    final = [(helped + j * PIECE, PIECE, helped // PIECE + smalls - 1 + j) for j in range(pieces - 1)]
    for k in range(smalls):
        final.append((rows_here - PIECE + k * SMALL, SMALL, wide + smalls - 2 + k))

    with scope("t_norms"):
        await_all(norms.at[pl.ds(0, grid_count - 2)], norm_recv.at[1])

        def source_scale(i):
            scales[i] = widen(bound(source(i))) * (1.0 / TOP)

        each(1, pairs, source_scale)

    with scope("t_lead2"):
        @pl.when(is_helper)
        def _():
            await_all(lead_came, lead_part_recv)

            def add(i):
                lead_sums[...] += lead_came[i - 1].astype(I32).astype(F32) * scales[i, 0:1, :]

            each(1, pairs, add)
            firsts[helped:rows_here, :] = solve(lead_sums[...] * lead_sums[...], c_high, c_low).astype(BF16)
            for target in (1, 2):
                for start, size, p in final:
                    chain(firsts, start, size, target, first_send, first_recv.at[p]).start()
            copy_to(lead_sums, lead_sums, sum_send, sum_recv, me, 0).start()

    def process(start, size, p, given):
        here = rows_at(start, size)

        def pass_on(buf, send_sem, recv_sem, lowest):
            @pl.when((rank >= lowest) & (rank < last))
            def _():
                chain(buf, start, size, rank + 1, send_sem, recv_sem.at[p]).start()

        def collect():
            await_all(came.at[:, here], part_recv.at[p])

            def add(i):
                out[here, :] += came[i - 1, here].astype(I32).astype(F32) * scales[i, 0:1, :]

            each(1, pairs, add)
            out[here, :] = out[here, :] * out[here, :]

        with scope("t_came"):
            if given:
                pl.when(rank > 0)(collect)
            else:
                collect()

        with scope("t_first"):
            @pl.when(rank == 0)
            def _():
                if given:
                    total = lead_sums[rows_at(start - helped, size), :]
                    out[here, :] = solve(total * total, a_high, a_low)
                else:
                    first = solve(out[here, :], a_high, a_low)
                    firsts[here] = first.astype(BF16)
                    out[here, :] = first

            def take():
                chain(firsts, start, size, rank, first_send, first_recv.at[p]).wait_recv()

            if given:
                pl.when((rank > 0) & (rank != HELPER))(take)
            else:
                pl.when(rank > 0)(take)
            pass_on(firsts, first_send, first_recv, HELPER if given else 0)

        with scope("t_second"):
            @pl.when(rank > 0)
            def _():
                out[here, :] -= apply(firsts[here], a_high, a_low)

            @pl.when(rank == 1)
            def _():
                second = solve(out[here, :], b_high, b_low)
                seconds[here] = second.astype(BF16)
                out[here, :] = second

            @pl.when(rank > 1)
            def _():
                chain(seconds, start, size, rank, second_send, second_recv.at[p]).wait_recv()

            pass_on(seconds, second_send, second_recv, 1)

        with scope("t_last"):
            @pl.when(rank > 1)
            def _():
                out[here, :] -= apply(seconds[here], b_high, b_low)

    @pl.loop(0, smalls)
    def _(k):
        process(k * SMALL, SMALL, k, False)

    @pl.loop(1, helped // PIECE)
    def _(p):
        q = lax.div(p, pieces) + 1

        @pl.when((lax.rem(p, pieces) == 1) & (rank == 0) & (q < chunks - 1))
        def _():
            send_parts(q, False)

        process(p * PIECE, PIECE, p + smalls - 1, False)

    @pl.when(rank == 0)
    def _():
        await_all(lead_sums, sum_recv)

    @pl.loop(helped // PIECE, wide - 1)
    def _(p):
        process(p * PIECE, PIECE, p + smalls - 1, True)

    @pl.loop(0, smalls)
    def _(k):
        process((wide - 1) * PIECE + k * SMALL, SMALL, wide + smalls - 2 + k, True)

    with scope("t_drain"):
        await_all(near, near_send)
        await_all(norms.at[pl.ds(0, grid_count - 1)], norm_send)
        point_copy(points, core, point_send, point_recv).wait_send()

        @pl.when(rank == 0)
        def _():
            await_all(sent.at[:, pl.ds(0, helped)], part_send)
            copy_to(index_v, lead_index, give_send.at[0], index_recv, me, HELPER).wait_send()
            await_all(low.at[pl.ds(0, half_rows)], give_send.at[1])

        @pl.when(rank > 0)
        def _():
            await_all(sent, part_send)

        @pl.when(is_helper)
        def _():
            await_all(low.at[pl.ds(0, half_rows)], swap_send)
            point_copy(lead_points, core, lead_point_send, lead_point_recv).wait_send()
            await_all(lead_sent, lead_part_send)
            await_all(lead_sums, sum_send)
            await_all(firsts.at[pl.ds(0, 2 * LANES)], first_send)

        @pl.when((rank < HELPER) | (is_helper & (rank < last)))
        def _():
            await_all(firsts.at[pl.ds(0, helped)], first_send)

        @pl.when(is_helper & (rank < last))
        def _():
            await_all(firsts.at[pl.ds(0, LANES)], first_send)

        @pl.when((rank > HELPER) & (rank < last))
        def _():
            await_all(firsts, first_send)

        @pl.when((rank > 0) & (rank < last))
        def _():
            await_all(seconds, second_send)


def on_device(grid_count, pt_count, orbitals, point_index, factor_panels):
    own_bands, grid_rows = orbitals.shape
    rows_here = grid_rows // grid_count
    panel = point_index.shape[0]
    chunks = rows_here // LANES
    pairs = grid_count // 2
    pieces = rows_here // PIECE + 2 * (PIECE // SMALL - 1)
    hbm = pl.BlockSpec(memory_space=pl.ANY)
    dma = pltpu.SemaphoreType.DMA
    square = [pltpu.VMEM((panel, panel), t) for t in (F32, F32, BF16, BF16, BF16, BF16)]
    scratch = [
        pltpu.VMEM((1, panel), I32),
        pltpu.VMEM((own_bands, grid_rows), BF16),
        pltpu.VMEM(factor_panels.shape, F32),
        pltpu.VMEM((chunks, own_bands, pairs * LANES), BF16),
        pltpu.VMEM((2, own_bands, panel), BF16),
        pltpu.VMEM((own_bands, panel), F32),
        pltpu.VMEM((BLOCK // SMALL, SMALL, panel), BF16),
        pltpu.VMEM((4, LANES, panel), F32),
        pltpu.VMEM((grid_count, 8, LANES), F32),
        pltpu.VMEM((pairs, 8, panel), F32),
        pltpu.VMEM((pairs - 1, rows_here, panel), I16),
        pltpu.VMEM((pairs - 1, rows_here, panel), I16),
        *square,
        pltpu.VMEM((rows_here, panel), BF16),
        pltpu.VMEM((rows_here, panel), BF16),
        pltpu.VMEM((1, panel), I32),
        pltpu.VMEM((2, own_bands, panel), BF16),
        pltpu.VMEM((pairs - 1, LANES, panel), I16),
        pltpu.VMEM((pairs - 1, LANES, panel), I16),
        pltpu.VMEM((LANES, panel), F32),
        pltpu.VMEM((panel, panel), BF16),
        pltpu.VMEM((panel, panel), BF16),
    ]
    used = sum(s.dtype.itemsize * functools.reduce(lambda a, b: a * b, s.shape) for s in scratch)
    sems = [
        dma((grid_rows // min(1024, grid_rows),)),
        dma, dma,
        dma, dma((2,)),
        dma, dma,
        dma, dma((2,)),
        *[dma, dma((pieces,))] * 3,
        dma((2,)), *[dma] * 10,
    ]
    args = [point_index.reshape(1, panel), orbitals, factor_panels]
    return pl.pallas_call(
        functools.partial(kernel, grid_count, pt_count),
        out_shape=jax.ShapeDtypeStruct((rows_here, panel), F32),
        in_specs=[hbm] * 3,
        out_specs=pl.BlockSpec(memory_space=pltpu.VMEM),
        scratch_shapes=scratch + sems,
        compiler_params=pltpu.CompilerParams(
            collective_id=0, has_side_effects=True, vmem_limit_bytes=min(used + 8 * 1024 * 1024, 64 * 1024 * 1024 - 1024 * 1024)
        ),
    )(*[pltpu.with_memory_space_constraint(a, pltpu.HBM) for a in args])


def solution(mesh):
    in_specs = (P("grid", None), P("pt"), P("pt", None))
    out_specs = P("grid", "pt")
    body = functools.partial(on_device, mesh.shape["grid"], mesh.shape["pt"])
    return jax.shard_map(
        body, mesh=mesh, in_specs=in_specs, out_specs=out_specs, check_vma=False
    )
```

time: 41.1 us -> 39.5 us (0.961)
  Pallas kernels: 39.4 us -> 37.9 us
    pallas_call x1, Pallas kernels: 39.4 us -> 37.9 us  [on_device(): pl.pallas_call(functools.partial(kernel, grid_count, pt_count), out_shape...]
where the time goes in v3:
time: 39.5 us; the launch traced here: 38.9 us
  Pallas kernels  37.9 us (96%)
  local copies, waits for them, and re-layouts  0.97 us (2%)
    pallas_call x1, Pallas kernels, on_device(): pl.pallas_call(functools.partial(kernel, grid_count, pt_count), out_shape...  37.9 us
    unnamed x1, local copies, waits for them, and re-layouts  0.97 us

profile of v3, /device:TPU:24, one launch (start us, length us, event | category | flops | bytes accessed | tf_op | source)
XLA Modules:
  0.0 38.9 jit_solution(16770680753167145787)
XLA Ops:
  0.0 37.9 %shard_map.37 = f32[512,512]{1,0:T(8,128)S(1)} custom-call(s32[1,512]{1,0:T(1,128)} %bitcast.1, bf16[256,4096]{1,0:T(8,128)(2,1)} %orb.1, f32[512,1024]{1,0:T(8,128)} %fac.1), custom_call_target="tpu_custom_call" | custom-call | tf_op jit(solution)/shard_map/pallas_call | solution.py:671
  37.9 1.0 %copy.5 = f32[512,512]{1,0:T(8,128)} copy(f32[512,512]{1,0:T(8,128)S(1)} %shard_map.37) | data formatting | bytes 2097152

commit v4 on v3

--- a/solution.py
+++ b/solution.py
@@ -96,11 +96,11 @@
     grid_count, pt_count, index, orb, fac, out,
     index_v, orb_v, fac_v, near, points, gathered, ramp, early, norms, scales, sent, came,
     low, inv, a_high, a_low, b_high, b_low, firsts, seconds,
-    lead_index, lead_points, lead_sent, lead_came, lead_sums, c_high, c_low,
+    lead_index, lead_points, lead_sent, lead_came, lead_sums, lead_code, lead_scale, c_high, c_low, relay_sent, relay_came, cross,
     load_sem, index_sem, fac_sem, near_send, near_recv, point_send, point_recv, norm_send, norm_recv,
     part_send, part_recv, first_send, first_recv, second_send, second_recv,
     give_send, index_recv, low_recv, swap_send, swap_recv, lead_point_send, lead_point_recv,
-    lead_part_send, lead_part_recv, sum_send, sum_recv,
+    lead_part_send, lead_part_recv, sum_send, sum_recv, relay_send, relay_recv, cross_send,
 ):
     me = lax.axis_index("grid")
     rank = lax.axis_index("pt")
@@ -121,6 +121,9 @@
     wide = rows_here // PIECE
     helped = rows_here - LANES
     is_helper = rank == HELPER
+    half = panel // 2
+    first_cross = chunks - 2
+    crossing = pairs == 4 and chunks >= 4
 
     def load(s):
         at = pl.ds(pl.multiple_of(s * depth, depth), depth)
@@ -157,6 +160,10 @@
     def _():
         greet(me, 0)
         greet(me, 1)
+
+    @pl.when((rank == 0) | (rank == 2))
+    def _():
+        greet(me, 2 - rank)
 
     steps_of = lax.broadcasted_iota(I32, (BLOCK, panel), 0).astype(F32).astype(BF16)
     ramp[...] = steps_of.reshape(ramp.shape)
@@ -197,6 +204,7 @@
         near_ranks = (
             jnp.where(rank > 0, 1, 0) + jnp.where(rank < last, 1, 0)
             + jnp.where(rank < 2, 1, 0) + jnp.where(is_helper, 2, 0)
+            + jnp.where((rank == 0) | (rank == 2), 1, 0)
         )
         for count in range(1, 5):
 
@@ -315,10 +323,10 @@
         scales[0] = TOP / widen(bound(chip))
         point_copy(points, 1 - core, point_send, point_recv).wait_recv()
 
-    def part_copy(start, size, p, i):
+    def part_copy(start, size, p, i, send_sem=part_send):
         return copy_to(
             sent.at[i - 1, rows_at(start, size)], came.at[i - 1, rows_at(start, size)],
-            part_send, part_recv.at[p], 2 * peer(i) + core, rank,
+            send_sem, part_recv.at[p], 2 * peer(i) + core, rank,
         )
 
     def send_rows(start, size, p):
@@ -379,8 +387,11 @@
             lead_points[core] = gathered[...].astype(BF16)
             point_copy(lead_points, core, lead_point_send, lead_point_recv).start()
 
+    def await_near():
+        await_all(near.at[pl.ds(1, chunks - 1)], near_recv.at[1])
+
     with scope("t_near"):
-        await_all(near.at[pl.ds(1, chunks - 1)], near_recv.at[1])
+        pl.when(rank > 0)(await_near)
 
     with scope("t_lead"):
         @pl.when(is_helper)
@@ -396,11 +407,34 @@
             each(1, pairs, lead_parts)
             lead_sums[...] = own_sums(chunks - 1, chip, lead_points) + near_sums(chunks - 1, chip, lead_points)
 
+    def relay_copy(t, side):
+        return copy_to(
+            relay_sent.at[t, side], relay_came.at[t, side], relay_send, relay_recv.at[t],
+            2 * peer(3 - side) + core, rank,
+        )
+
+    def cross_parts(t):
+        q = first_cross + t
+        code = encode(own_sums(q, peer(1), points) + near_sums(q, peer(1), points))
+        relay_sent[t, 0] = code[:, :half]
+        relay_sent[t, 1] = code[:, half:]
+        relay_copy(t, 0).start()
+        relay_copy(t, 1).start()
+        for i in range(2):
+            early[2 * t + i] = own_sums(q, peer(2 + i), points) + near_sums(q, peer(2 + i), points)
+        out[rows_of(q), :] = own_sums(q, chip, points) + near_sums(q, chip, points)
+
     @pl.when(rank > 0)
     def _():
-        @pl.loop(1, chunks)
+        if crossing:
+            cross_parts(0)
+
+        @pl.loop(1, first_cross if crossing else chunks)
         def _(q):
             send_parts(q, False)
+
+        if crossing:
+            cross_parts(1)
 
     with scope("t_invert"):
         load_fac.wait()
@@ -447,8 +481,6 @@
         part = buf.at[rows_at(start, size)]
         return copy_to(part, part, send_sem, recv_sem, me, target)
 
-    half = panel // 2
-
     def solve(value, high, low_part):
         size = value.shape[0]
         value_high, value_low = split(value)
@@ -469,6 +501,8 @@
     for k in range(smalls):
         final.append((rows_here - PIECE + k * SMALL, SMALL, wide + smalls - 2 + k))
 
+    pl.when(rank == 0)(await_near)
+
     with scope("t_norms"):
         await_all(norms.at[pl.ds(0, grid_count - 2)], norm_recv.at[1])
 
@@ -476,6 +510,26 @@
             scales[i] = widen(bound(source(i))) * (1.0 / TOP)
 
         each(1, pairs, source_scale)
+
+        if crossing:
+            away, up, over = bound(peer(1)), bound(peer(2)), bound(peer(3))
+            here_only = scales[0]
+            cross[0, :, :half] = (TOP / widen(bound(chip) + over))[:, :half]
+            cross[0, :, half:] = here_only[:, half:]
+            cross[1, :, :half] = here_only[:, :half]
+            cross[1, :, half:] = (TOP / widen(bound(chip) + up))[:, half:]
+            cross[2, :, :half] = (widen(up + away) * (1.0 / TOP))[:, :half]
+            cross[2, :, half:] = scales[2][:, half:]
+            cross[3, :, :half] = scales[3][:, :half]
+            cross[3, :, half:] = (widen(over + away) * (1.0 / TOP))[:, half:]
+
+        lead_scale[...] = jnp.broadcast_to(bound(chip), lead_scale.shape)
+
+        def include(i):
+            lead_scale[...] += jnp.broadcast_to(bound(source(i)), lead_scale.shape)
+
+        each(1, pairs, include)
+        lead_scale[...] = jnp.maximum(lead_scale[...], 1e-30)
 
     with scope("t_lead2"):
         @pl.when(is_helper)
@@ -490,13 +544,47 @@
             for target in (1, 2):
                 for start, size, p in final:
                     chain(firsts, start, size, target, first_send, first_recv.at[p]).start()
-            copy_to(lead_sums, lead_sums, sum_send, sum_recv, me, 0).start()
-
-    def process(start, size, p, given):
+            lead_code[...] = jnp.round(lead_sums[...] * (TOP / lead_scale[0:1, :])).astype(I32).astype(I16)
+            copy_to(lead_code, lead_code, sum_send, sum_recv, me, 0).start()
+
+    def relay(t):
+        q = first_cross + t
+        await_all(relay_came.at[t], relay_recv.at[t])
+
+        def add(side, columns):
+            value = relay_came[t, side].astype(I32).astype(F32) * scales[3 - side, 0:1, columns]
+            early[2 * t + side, :, columns] += value
+
+        add(0, slice(0, half))
+        add(1, slice(half, panel))
+        for i in range(2):
+            value = early[2 * t + i] * cross[i, 0:1, :]
+            sent[1 + i, rows_of(q)] = jnp.round(value).astype(I32).astype(I16)
+        parts = final if t == 1 else [
+            (q * LANES + j * PIECE, PIECE, q * pieces + smalls - 1 + j) for j in range(pieces)
+        ]
+        for start, size, p in parts:
+            for i in (2, 3):
+                part_copy(start, size, p, i, cross_send).start()
+
+    def lead_ahead():
+        for start, size, p in final:
+
+            @pl.when(rank != HELPER)
+            def _():
+                chain(firsts, start, size, rank, first_send, first_recv.at[p]).wait_recv()
+
+            @pl.when((rank >= HELPER) & (rank < last))
+            def _():
+                chain(firsts, start, size, rank + 1, first_send, first_recv.at[p]).start()
+
+        lead_sums[...] = apply(firsts[helped:rows_here, :], a_high, a_low)
+
+    def process(start, size, p, given, crossed=False, straight=False):
         here = rows_at(start, size)
 
-        def pass_on(buf, send_sem, recv_sem, lowest):
-            @pl.when((rank >= lowest) & (rank < last))
+        def pass_on(buf, send_sem, recv_sem, skipped):
+            @pl.when((rank < last) & jnp.logical_not(skipped))
             def _():
                 chain(buf, start, size, rank + 1, send_sem, recv_sem.at[p]).start()
 
@@ -509,36 +597,50 @@
             each(1, pairs, add)
             out[here, :] = out[here, :] * out[here, :]
 
+        def collect_cross():
+            await_all(came.at[pl.ds(1, 2), here], part_recv.at[p])
+            for i in range(2):
+                out[here, :] += came[1 + i, here].astype(I32).astype(F32) * cross[2 + i, 0:1, :]
+            out[here, :] = out[here, :] * out[here, :]
+
         with scope("t_came"):
-            if given:
-                pl.when(rank > 0)(collect)
+            if not crossed:
+                collect()
             else:
-                collect()
+                pl.when(rank > 0)(collect_cross if crossing else collect)
+                if not given:
+                    pl.when(rank == 0)(collect)
 
         with scope("t_first"):
             @pl.when(rank == 0)
             def _():
                 if given:
-                    total = lead_sums[rows_at(start - helped, size), :]
+                    total = lead_code[rows_at(start - helped, size), :].astype(I32).astype(F32)
+                    total = total * (lead_scale[0:1, :] * (1.0 / TOP))
                     out[here, :] = solve(total * total, a_high, a_low)
                 else:
                     first = solve(out[here, :], a_high, a_low)
                     firsts[here] = first.astype(BF16)
                     out[here, :] = first
 
-            def take():
-                chain(firsts, start, size, rank, first_send, first_recv.at[p]).wait_recv()
-
-            if given:
-                pl.when((rank > 0) & (rank != HELPER))(take)
-            else:
-                pl.when(rank > 0)(take)
-            pass_on(firsts, first_send, first_recv, HELPER if given else 0)
+            if not given:
+                @pl.when(rank > 0)
+                def _():
+                    chain(firsts, start, size, rank, first_send, first_recv.at[p]).wait_recv()
+
+                pass_on(firsts, first_send, first_recv, (rank == 1) & straight)
+
+                @pl.when((rank == 0) & straight)
+                def _():
+                    chain(firsts, start, size, 2, first_send, first_recv.at[p]).start()
 
         with scope("t_second"):
             @pl.when(rank > 0)
             def _():
-                out[here, :] -= apply(firsts[here], a_high, a_low)
+                if given:
+                    out[here, :] -= lead_sums[rows_at(start - helped, size), :]
+                else:
+                    out[here, :] -= apply(firsts[here], a_high, a_low)
 
             @pl.when(rank == 1)
             def _():
@@ -550,7 +652,7 @@
             def _():
                 chain(seconds, start, size, rank, second_send, second_recv.at[p]).wait_recv()
 
-            pass_on(seconds, second_send, second_recv, 1)
+            pass_on(seconds, second_send, second_recv, rank == 0)
 
         with scope("t_last"):
             @pl.when(rank > 1)
@@ -559,9 +661,11 @@
 
     @pl.loop(0, smalls)
     def _(k):
-        process(k * SMALL, SMALL, k, False)
-
-    @pl.loop(1, helped // PIECE)
+        process(k * SMALL, SMALL, k, False, False, True)
+
+    begin = first_cross * pieces
+
+    @pl.loop(1, begin)
     def _(p):
         q = lax.div(p, pieces) + 1
 
@@ -569,19 +673,34 @@
         def _():
             send_parts(q, False)
 
-        process(p * PIECE, PIECE, p + smalls - 1, False)
+        process(p * PIECE, PIECE, p + smalls - 1, False, False, p < 2)
+
+        if crossing:
+            for t, due in ((0, pieces), (1, 2 * pieces - 1)):
+
+                @pl.when((rank > 0) & (p == due))
+                def _():
+                    relay(t)
+
+    @pl.loop(begin, helped // PIECE)
+    def _(p):
+        @pl.when((p == helped // PIECE - 1) & (rank > 0))
+        def _():
+            lead_ahead()
+
+        process(p * PIECE, PIECE, p + smalls - 1, False, True)
 
     @pl.when(rank == 0)
     def _():
-        await_all(lead_sums, sum_recv)
+        await_all(lead_code, sum_recv)
 
     @pl.loop(helped // PIECE, wide - 1)
     def _(p):
-        process(p * PIECE, PIECE, p + smalls - 1, True)
+        process(p * PIECE, PIECE, p + smalls - 1, True, True)
 
     @pl.loop(0, smalls)
     def _(k):
-        process((wide - 1) * PIECE + k * SMALL, SMALL, wide + smalls - 2 + k, True)
+        process((wide - 1) * PIECE + k * SMALL, SMALL, wide + smalls - 2 + k, True, True)
 
     with scope("t_drain"):
         await_all(near, near_send)
@@ -596,17 +715,29 @@
 
         @pl.when(rank > 0)
         def _():
-            await_all(sent, part_send)
+            if crossing:
+                direct = first_cross * LANES
+                await_all(sent.at[:, pl.ds(0, direct)], part_send)
+                await_all(sent.at[pl.ds(1, 2), pl.ds(direct, rows_here - direct)], cross_send)
+                await_all(relay_sent, relay_send)
+            else:
+                await_all(sent, part_send)
 
         @pl.when(is_helper)
         def _():
             await_all(low.at[pl.ds(0, half_rows)], swap_send)
             point_copy(lead_points, core, lead_point_send, lead_point_recv).wait_send()
             await_all(lead_sent, lead_part_send)
-            await_all(lead_sums, sum_send)
+            await_all(lead_code, sum_send)
             await_all(firsts.at[pl.ds(0, 2 * LANES)], first_send)
 
-        @pl.when((rank < HELPER) | (is_helper & (rank < last)))
+        for at, count in ((0, helped + 2 * PIECE), (1, helped - 2 * PIECE), (2, helped)):
+
+            @pl.when(rank == at)
+            def _():
+                await_all(firsts.at[pl.ds(0, count)], first_send)
+
+        @pl.when(is_helper & (rank < last))
         def _():
             await_all(firsts.at[pl.ds(0, helped)], first_send)
 
@@ -654,8 +785,13 @@
         pltpu.VMEM((pairs - 1, LANES, panel), I16),
         pltpu.VMEM((pairs - 1, LANES, panel), I16),
         pltpu.VMEM((LANES, panel), F32),
+        pltpu.VMEM((LANES, panel), I16),
+        pltpu.VMEM((8, panel), F32),
         pltpu.VMEM((panel, panel), BF16),
         pltpu.VMEM((panel, panel), BF16),
+        pltpu.VMEM((2, 2, LANES, panel // 2), I16),
+        pltpu.VMEM((2, 2, LANES, panel // 2), I16),
+        pltpu.VMEM((4, 8, panel), F32),
     ]
     used = sum(s.dtype.itemsize * functools.reduce(lambda a, b: a * b, s.shape) for s in scratch)
     sems = [
@@ -665,7 +801,8 @@
         dma, dma,
         dma, dma((2,)),
         *[dma, dma((pieces,))] * 3,
-        dma((2,)), *[dma] * 10,
+        dma((2,)), *[dma] * 11,
+        dma((2,)), dma,
     ]
     args = [point_index.reshape(1, panel), orbitals, factor_panels]
     return pl.pallas_call(

time: 39.5 us -> 38.7 us (0.980)
  Pallas kernels: 37.9 us -> 37.4 us
    pallas_call x1, Pallas kernels: 37.9 us -> 37.4 us  [on_device(): pl.pallas_call(functools.partial(kernel, grid_count, pt_count), out_shape...]
where the time goes in v4:
time: 38.7 us; the launch traced here: 38.4 us
  Pallas kernels  37.4 us (97%)
  local copies, waits for them, and re-layouts  0.97 us (3%)
    pallas_call x1, Pallas kernels, on_device(): pl.pallas_call(functools.partial(kernel, grid_count, pt_count), out_shape...  37.4 us
    unnamed x1, local copies, waits for them, and re-layouts  0.97 us

profile of v4, /device:TPU:24, one launch (start us, length us, event | category | flops | bytes accessed | tf_op | source)
XLA Modules:
  0.0 38.4 jit_solution(8735738583264157057)
XLA Ops:
  0.0 37.4 %shard_map.37 = f32[512,512]{1,0:T(8,128)S(1)} custom-call(s32[1,512]{1,0:T(1,128)} %bitcast.1, bf16[256,4096]{1,0:T(8,128)(2,1)} %orb.1, f32[512,1024]{1,0:T(8,128)} %fac.1), custom_call_target="tpu_custom_call" | custom-call | tf_op jit(solution)/shard_map/pallas_call | solution.py:808
  37.4 1.0 %copy.5 = f32[512,512]{1,0:T(8,128)} copy(f32[512,512]{1,0:T(8,128)S(1)} %shard_map.37) | data formatting | bytes 2097152
